TPU v7x, 256 devices: a whole 4x4x8 slice. The times are simulated.
256 devices in a mesh: seq: 32 (over z, x_hi, core), tp: 8 (over x_lo, y).
Axes of the slice: x: 4 (x_hi: 2, x_lo: 2; x = x_hi * 2 + x_lo), y: 4, z: 8, core: 2. Of those that a mesh axis runs over, the one named last changes fastest.
Arguments:
- query: bfloat16 [8192, 3584], P('seq', 'tp'), may hold values from -6 to 6
- keys: bfloat16 [8192, 3584], P('seq', 'tp'), may hold values from -6 to 6
- values: bfloat16 [8192, 3584], P('seq', 'tp'), may hold values from -6 to 6
- prefix_keys: bfloat16 [4096, 3584], P('seq', 'tp'), may hold values from -6 to 6
- prefix_values: bfloat16 [4096, 3584], P('seq', 'tp'), may hold values from -6 to 6
- residual: bfloat16 [8192, 3584], P('seq', 'tp'), may hold values from -4 to 4
- out_weight: bfloat16 [3584, 3584], P('tp'), may hold values from -1 to 1
- suffix_lens: int32 [16], replicated, may hold values from 1 to 2048, 8192 in all
- req_group: int32 [16], replicated, may hold values from 0 to 3
- placement: int32 [8192], replicated, may hold values from 0 to 8191, each once
- prefix_owner: int32 [32], replicated, may hold values from 0 to 3, as said below
Outputs:
- hidden: bfloat16 [8192, 3584], P('seq', 'tp')
- cache_keys: bfloat16 [8192, 3584], P('seq', 'tp')
- cache_values: bfloat16 [8192, 3584], P('seq', 'tp')
Inputs may be any that keep to these rules, and one draw needn't show every extreme that they name: `prefix_owner`: each group number appears exactly 8 times.
All inputs are finite; a program needn't handle non-finite values.
Results may differ from a plain program's by a relative error of at most 0.014.
Values may be sent and summed in bfloat16 or wider, within the bound.
A program may use at most 128 MiB of HBM per device.

v0:
```python
import math

import jax
import jax.numpy as jnp
from jax import lax
from jax.sharding import PartitionSpec as P

HD = 224


NEG_FILL = -1e30


def request_of(positions, ends):
    return jnp.sum((positions[:, None] >= ends[None, :]).astype(jnp.int32), axis=1)


def lookup_small(indices, table):
    slots = jnp.arange(table.shape[0], dtype=jnp.int32)
    return jnp.sum(jnp.where(indices[:, None] == slots[None, :], table[None, :], 0), axis=1)


def absorb(state, query_heads, key_piece, value_piece, visible):
    top, total, accum = state
    count = key_piece.shape[0]
    heads = query_heads.shape[1]
    head_size = query_heads.shape[2]
    key_heads = key_piece.reshape(count, heads, head_size)
    value_heads = value_piece.reshape(count, heads, head_size)
    scores = jnp.einsum(
        "qhd,khd->hqk", query_heads, key_heads, preferred_element_type=jnp.float32
    ) * (1.0 / math.sqrt(head_size))
    scores = jnp.where(visible[None], scores, NEG_FILL)
    fresh = jnp.maximum(top, jnp.max(scores, axis=2))
    weights = jnp.where(visible[None], jnp.exp(scores - fresh[:, :, None]), 0.0).astype(
        jnp.bfloat16
    )
    factor = jnp.exp(top - fresh)
    total = factor * total + jnp.sum(weights.astype(jnp.float32), axis=2)
    accum = factor[:, :, None] * accum + jnp.einsum(
        "hqk,khd->hqd", weights, value_heads, preferred_element_type=jnp.float32
    )
    return (fresh, total, accum)


def shards(
    query,
    keys,
    values,
    prefix_keys,
    prefix_values,
    residual,
    out_weight,
    suffix_lens,
    req_group,
    placement,
    prefix_owner,
):
    rows, width = query.shape
    block_rows = prefix_keys.shape[0]
    heads = width // HD
    me = lax.axis_index("seq")
    ends = jnp.cumsum(suffix_lens)
    my_pos = lax.dynamic_slice_in_dim(placement, me * rows, rows)
    my_req = request_of(my_pos, ends)
    my_grp = lookup_small(my_req, req_group)
    query_heads = query.reshape(rows, heads, HD)
    start_state = (
        jnp.full((heads, rows), NEG_FILL, jnp.float32),
        jnp.zeros((heads, rows), jnp.float32),
        jnp.zeros((heads, rows, HD), jnp.float32),
    )
    empty_cache = jnp.zeros((rows, width), jnp.bfloat16)
    pieces = (
        lax.all_gather(keys, "seq", axis=0, tiled=True),
        lax.all_gather(values, "seq", axis=0, tiled=True),
    )
    state = start_state
    cache = (empty_cache, empty_cache)
    count = pieces[0].shape[0]
    valid = jnp.ones((count,), jnp.bool_)
    key_req = request_of(placement, ends)
    state = absorb(
        state,
        query_heads,
        pieces[0],
        pieces[1],
        valid[None, :]
        & (key_req[None, :] == my_req[:, None])
        & (placement[None, :] <= my_pos[:, None]),
    )
    local = placement - me * rows
    keep = valid & (local >= 0) & (local < rows)
    target = jnp.where(keep, local, rows)
    cache = (
        cache[0].at[target].set(pieces[0], mode="drop"),
        cache[1].at[target].set(pieces[1], mode="drop"),
    )
    state, cache = (state, cache)
    pieces = (
        lax.all_gather(prefix_keys, "seq", axis=0, tiled=True),
        lax.all_gather(prefix_values, "seq", axis=0, tiled=True),
    )
    count = pieces[0].shape[0]
    key_block = jnp.arange(count, dtype=jnp.int32) // block_rows
    valid = jnp.ones((count,), jnp.bool_)
    key_grp = lookup_small(key_block, prefix_owner)
    state = absorb(
        state,
        query_heads,
        pieces[0],
        pieces[1],
        valid[None, :] & (key_grp[None, :] == my_grp[:, None]),
    )
    top, total, accum = state
    attended = accum / total[:, :, None]
    attended = jnp.transpose(attended, (1, 0, 2)).reshape(rows, width).astype(jnp.bfloat16)
    term = jnp.dot(attended, out_weight, preferred_element_type=jnp.float32)
    summed = lax.psum_scatter(
        term.astype(jnp.bfloat16), "tp", scatter_dimension=1, tiled=True
    ).astype(jnp.float32)
    hidden = (residual.astype(jnp.float32) + summed).astype(jnp.bfloat16)
    return (hidden, cache[0], cache[1])


def solution(mesh):
    return jax.shard_map(
        shards,
        mesh=mesh,
        in_specs=(
            P("seq", "tp"),
            P("seq", "tp"),
            P("seq", "tp"),
            P("seq", "tp"),
            P("seq", "tp"),
            P("seq", "tp"),
            P("tp", None),
            P(),
            P(),
            P(),
            P(),
        ),
        out_specs=(P("seq", "tp"), P("seq", "tp"), P("seq", "tp")),
        check_vma=False,
    )
```

profile of v0, /device:TPU:1, one launch (start us, length us, event | category | flops | bytes accessed | tf_op | source)
XLA Modules:
  0.0 508.1 jit_solution(1577933013104015989)
XLA Ops:
  10.9 0.8 dynamic_slice.3
  11.8 0.7 select_reduce_fusion.1
  12.5 0.9 convert_reduce_fusion.2
  13.4 0.8 select_reduce_fusion
  14.3 1.6 broadcast_compare_fusion
  15.9 3.6 compare_and_fusion
  19.4 79.9 %all-gather.7.cloned.1.call-done = bf16[4096,448]{0,1:T(8,128)(2,1)} async-done(((bf16[128,448]{0,1:T(8,128)(2,1)}), bf16[4096,448]{0,1:T(8,128)(2,1)}) %all-gather.7.cloned.1.call-update) | async-done | bytes 3670032 | tf_op jit(solution)/shard_map/all_gather | solution.py:101
  99.3 7.9 %fusion.1 = (f32[2,256]{1,0:T(2,128)S(1)}, f32[2,256,4096]{2,1,0:T(8,128)}) fusion(pred[256,4096]{1,0:T(8,128)(4,1)} %broadcast_compare_fusion, bf16[256,2,224]{0,2,1:T(8,128)(2,1)} %bitcast.56, bf16[4096,2,224]{0,2,1:T(8,128)(2,1)} %bitcast.55), kind=kOutput, calls=%fused_computation.10 | convolution fusion | flops 945815040 | bytes 13338624 | tf_op jit(solution)/shard_map/qhd,khd->hqk/dot_general | solution.py:30
  107.2 94.4 %all-gather.5.cloned.1.call-done = bf16[8192,448]{0,1:T(8,128)(2,1)} async-done(((bf16[256,448]{0,1:T(8,128)(2,1)}), bf16[8192,448]{0,1:T(8,128)(2,1)}) %all-gather.5.cloned.1.call-update) | async-done | bytes 7340048 | tf_op jit(solution)/shard_map/all_gather | solution.py:75
  201.6 12.2 %fusion = (f32[2,256]{1,0:T(2,128)S(1)}, f32[2,256,8192]{2,1,0:T(8,128)}) fusion(pred[256,8192]{1,0:T(8,128)(4,1)} %compare_and_fusion, bf16[256,2,224]{0,2,1:T(8,128)(2,1)S(1)} %bitcast.57, bf16[8192,2,224]{0,2,1:T(8,128)(2,1)} %bitcast.50), kind=kOutput, calls=%fused_computation.5 | convolution fusion | flops 1891630592 | bytes 26445824 | tf_op jit(solution)/shard_map/qhd,khd->hqk/dot_general | solution.py:30
  213.9 2.7 convert_reduce_fusion.1
  216.5 8.6 %convert_reduce_fusion = f32[2,256]{1,0:T(2,128)S(1)} fusion(f32[2,256]{1,0:T(2,128)S(1)} %get-tuple-element.12, f32[2,256,8192]{2,1,0:T(8,128)} %get-tuple-element.15, pred[256,8192]{1,0:T(8,128)(4,1)S(1)} %copy-done.1), kind=kLoop, calls=%fused_computation.2 | loop fusion | flops 29359616 | bytes 18878464 | tf_op jit(solution)/shard_map/reduce_sum | solution.py:39
  225.1 59.9 %all-gather.11.cloned.1.call-done = bf16[4096,448]{0,1:T(8,128)(2,1)} async-done(((bf16[128,448]{0,1:T(8,128)(2,1)}), bf16[4096,448]{0,1:T(8,128)(2,1)}) %all-gather.11.cloned.1.call-update) | async-done | bytes 3670032 | tf_op jit(solution)/shard_map/all_gather | solution.py:102
  285.0 7.7 %convolution_bitcast_fusion = f32[256,2,224]{0,2,1:T(8,128)} fusion(bf16[4096,2,224]{0,2,1:T(8,128)(2,1)} %bitcast.54, f32[2,256,4096]{2,1,0:T(8,128)} %get-tuple-element.17, f32[2,256]{1,0:T(2,128)S(1)} %get-tuple-element.13, pred[256,4096]{1,0:T(8,128)(4,1)} %broadcast_compare_fusion), kind=kOutput, calls=%fused_computation.13 | convolution fusion | flops 950009856 | bytes 13568000 | tf_op jit(solution)/shard_map/hqk,khd->hqd/dot_general | solution.py:40
  292.8 94.4 %all-gather.9.cloned.1.call-done = bf16[8192,448]{0,1:T(8,128)(2,1)} async-done(((bf16[256,448]{0,1:T(8,128)(2,1)}), bf16[8192,448]{0,1:T(8,128)(2,1)}) %all-gather.9.cloned.1.call-update) | async-done | bytes 7340048 | tf_op jit(solution)/shard_map/all_gather | solution.py:76
  387.2 13.2 %fusion.6 = bf16[256,2,224]{0,2,1:T(8,128)(2,1)S(1)} fusion(f32[256,2,224]{0,2,1:T(8,128)} %convolution_bitcast_fusion, bf16[8192,2,224]{0,2,1:T(8,128)(2,1)} %bitcast.51, f32[256,2]{0,1:T(2,128)S(1)} %get-tuple-element.9, f32[256,2]{0,1:T(2,128)S(1)} %get-tuple-element.11, f32[256,2]{0,1:T(2,128)S(1)} %get-tuple-element.10, ...), kind=kOutput, calls=%fused_computation.19 | convolution fusion | flops 1900593152 | bytes 26910720 | tf_op jit(solution)/shard_map/hqk,khd->hqd/dot_general | solution.py:40
  400.4 2.9 convolution_convert_fusion
  403.3 11.6 %copy.21 = bf16[8192,448]{1,0:T(8,128)(2,1)} copy(bf16[8192,448]{0,1:T(8,128)(2,1)} %all-gather.5.cloned.1.call-done) | data formatting | bytes 14680064 | tf_op jit(solution)/shard_map/all_gather | solution.py:75
  414.9 35.8 %scatter_custom_fusion = bf16[256,448]{1,0:T(8,128)(2,1)S(1)} fusion(s32[8192]{0:T(1024)S(1)} %compare_select_fusion, bf16[8192,448]{1,0:T(8,128)(2,1)} %copy.21, bf16[]{:T(256)} %constant.47.clone.1), kind=kCustom, calls=%fused_computation.26 | custom fusion | bytes 229888 | tf_op jit(solution)/shard_map/scatter | solution.py:96
  450.7 0.8 copy.23
  451.5 11.6 %copy.22 = bf16[8192,448]{1,0:T(8,128)(2,1)} copy(bf16[8192,448]{0,1:T(8,128)(2,1)} %all-gather.9.cloned.1.call-done) | data formatting | bytes 14680064 | tf_op jit(solution)/shard_map/all_gather | solution.py:76
  463.1 35.8 %scatter_custom_fusion.1 = bf16[256,448]{1,0:T(8,128)(2,1)S(1)} fusion(s32[8192]{0:T(1024)S(1)} %compare_select_fusion, bf16[8192,448]{1,0:T(8,128)(2,1)} %copy.22, bf16[]{:T(256)} %constant.47.clone.1), kind=kCustom, calls=%fused_computation.24 | custom fusion | bytes 229888 | tf_op jit(solution)/shard_map/scatter | solution.py:97
  498.9 0.8 copy.24
  499.8 1.8 add_convert_fusion
  (31 shorter events, 3.8 us)
Async XLA Ops:
  7.2 393.2 %copy-start = (bf16[448,3584]{1,0:T(8,128)(2,1)S(1)}, bf16[448,3584]{1,0:T(8,128)(2,1)}, u32[]{:S(2)}) copy-start(bf16[448,3584]{1,0:T(8,128)(2,1)} %param.17) | copy-start | bytes 9633796
  7.2 92.1 %all-gather.7.cloned.1.call-start = ((), (), s32[]{:S(2)}) async-start(), calls=%async_computation.2 | async-start | bytes 3784704 | tf_op jit(solution)/shard_map/all_gather | solution.py:101
  7.9 193.7 %all-gather.5.cloned.1.call-start = ((), (), s32[]{:S(2)}) async-start(), calls=%async_computation.1 | async-start | bytes 7569408 | tf_op jit(solution)/shard_map/all_gather | solution.py:75
  8.7 276.4 %all-gather.11.cloned.1.call-start = ((), (), s32[]{:S(2)}) async-start(), calls=%async_computation.4 | async-start | bytes 3784704 | tf_op jit(solution)/shard_map/all_gather | solution.py:102
  9.4 377.8 %all-gather.9.cloned.1.call-start = ((), (), s32[]{:S(2)}) async-start(), calls=%async_computation.3 | async-start | bytes 7569408 | tf_op jit(solution)/shard_map/all_gather | solution.py:76
  10.0 489.8 %reduce-scatter.2.cloned.1.call-start = ((), (), s32[]{:S(2)}) async-start(), calls=%async_computation.5 | async-start | bytes 2064384 | tf_op jit(solution)/shard_map/reduce_scatter | solution.py:119
  19.4 182.1 %copy-start.5 = (bf16[256,448]{0,1:T(8,128)(2,1)S(1)}, bf16[256,448]{0,1:T(8,128)(2,1)}, u32[]{:S(2)}) copy-start(bf16[256,448]{0,1:T(8,128)(2,1)} %param.11) | copy-start | bytes 688132
  201.6 12.3 %copy-start.2 = (f32[2,256,4096]{2,1,0:T(8,128)S(1)}, f32[2,256,4096]{2,1,0:T(8,128)}, u32[]{:S(2)}) copy-start(f32[2,256,4096]{2,1,0:T(8,128)} %get-tuple-element.17) | copy-start | bytes 25165828
  201.6 12.3 %copy-start.3 = (pred[256,4096]{1,0:T(8,128)(4,1)S(1)}, pred[256,4096]{1,0:T(8,128)(4,1)}, u32[]{:S(2)}) copy-start(pred[256,4096]{1,0:T(8,128)(4,1)} %broadcast_compare_fusion) | copy-start | bytes 3145732
  213.8 2.7 copy-start.1
  387.2 16.1 %copy-start.4 = (s32[8192]{0:T(1024)S(1)}, s32[8192]{0:T(1024)}, u32[]{:S(2)}) copy-start(s32[8192]{0:T(1024)} %param.20) | copy-start | bytes 98308
Sparse Core Ops, SparseCore 0:
  10.6 88.6 all-gather.6
  101.8 99.6 all-gather.4
  204.1 80.8 all-gather.10
  287.5 99.6 all-gather.8
  403.4 35.0 reduce-scatter.1
where the time goes:
time: 509 us; the launch traced here: 508 us
  waiting for transfers between devices  331 us (65%)
  local copies, waits for them, and re-layouts  98 us (19%)
  matrix products  43.9 us (9%)
  other arithmetic  21 us (4%)
  between operations  13.9 us (3%)
    all_gather x1, waiting for transfers between devices, shards(): lax.all_gather(values, 'seq', axis=0, tiled=True)  94.4 us
    all_gather x1, waiting for transfers between devices, shards(): lax.all_gather(keys, 'seq', axis=0, tiled=True)  94.4 us
    all_gather x1, waiting for transfers between devices, shards(): lax.all_gather(prefix_keys, 'seq', axis=0, tiled=True)  79.9 us
    all_gather x1, waiting for transfers between devices, shards(): lax.all_gather(prefix_values, 'seq', axis=0, tiled=True)  59.9 us
    scatter x1, local copies, waits for them, and re-layouts, shards(): cache[0].at[target].set(pieces[0], mode='drop')  35.8 us
    scatter x1, local copies, waits for them, and re-layouts, shards(): cache[1].at[target].set(pieces[1], mode='drop')  35.8 us
    dot_general x2, matrix products, absorb(): jnp.einsum('hqk,khd->hqd', weights, value_heads, preferred_element_type=j...  20.9 us
    dot_general x2, matrix products, absorb(): jnp.einsum('qhd,khd->hqk', query_heads, key_heads, preferred_element_type...  20.1 us
  transfers between devices with their start and end apart: 5, of which 4 were waited for; matrix products, arithmetic and copies ran while one was open for 29% of the time, Pallas kernels for 0%

commit v1 on v0

v1 whole, which is shorter than its diff:
```python
import math

import jax
import jax.numpy as jnp
from jax import lax
from jax.experimental import pallas as pl
from jax.experimental.pallas import tpu as pltpu
from jax.sharding import PartitionSpec as P

HD = 224
ROWS = 256
PBLK = 128
PART = ROWS + PBLK
LANES = 2 * PART
QN = 2 * ROWS
KV = 2 * HD
AUG = KV + 16
NZ = 8
TQ = 256
NEG = -1e30
COEF = math.log2(math.e) / math.sqrt(HD)
MESH = pl.DeviceIdType.MESH
NT = (((1,), (1,)), ((), ()))


def attention_kernel(
    lens_ref,
    group_ref,
    owner_ref,
    pos_ref,
    q_ref,
    k_ref,
    v_ref,
    pk_ref,
    pv_ref,
    att_ref,
    ck_ref,
    cv_ref,
    gathered,
    q_other,
    q_rows,
    q_pos,
    q_start,
    q_grp,
    top,
    accum,
    cache,
    att_send,
    cache_send,
    att_recv,
    cache_recv,
    ring_send,
    ring_recv,
    twin_send,
    twin_recv,
    pair_send,
    pair_recv,
):
    seq = lax.axis_index("seq")
    tp = lax.axis_index("tp")
    z = seq // 4
    xh = (seq // 2) % 2
    core = seq % 2
    other = 1 - xh
    twin = 1 - core

    def dev(zz, xx, cc):
        return (zz * 4 + xx * 2 + cc, tp)

    up = dev(lax.rem(z + 1, NZ), xh, core)
    down = dev(lax.rem(z + NZ - 1, NZ), xh, core)
    pair = dev(z, other, core)
    sibling = dev(z, xh, twin)

    barrier = pltpu.get_barrier_semaphore()
    for peer in (up, down, pair, sibling):
        pl.semaphore_signal(barrier, inc=1, device_id=peer, device_id_type=MESH)
    pl.semaphore_wait(barrier, 4)

    mine = pl.multiple_of(xh * HD, 32)
    theirs = pl.multiple_of(other * HD, 32)
    mine_lane = pl.multiple_of(xh * PART, 128)
    theirs_lane = pl.multiple_of(other * PART, 128)

    def remote(src, dst, send, recv, device):
        return pltpu.make_async_remote_copy(
            src_ref=src,
            dst_ref=dst,
            send_sem=send,
            recv_sem=recv,
            device_id=device,
            device_id_type=MESH,
        )

    home = gathered.at[z, core]

    def pair_copies():
        pairs = (
            (k_ref, 0, 0, ROWS),
            (pk_ref, 0, ROWS, PBLK),
            (v_ref, HD, 0, ROWS),
            (pv_ref, HD, ROWS, PBLK),
        )
        copies = [
            remote(
                ref.at[pl.ds(theirs, HD)],
                home.at[pl.ds(row, HD), pl.ds(pl.multiple_of(mine_lane + lane, 128), width)],
                pair_send.at[i],
                pair_recv.at[i],
                pair,
            )
            for i, (ref, row, lane, width) in enumerate(pairs)
        ]
        copies.append(
            remote(q_ref.at[pl.ds(theirs, HD)], q_other, pair_send.at[4], pair_recv.at[4], pair)
        )
        return copies

    exchange = pair_copies()
    for copy in exchange:
        copy.start()

    for ref, row, lane, width in (
        (k_ref, 0, 0, ROWS),
        (pk_ref, 0, ROWS, PBLK),
        (v_ref, HD, 0, ROWS),
        (pv_ref, HD, ROWS, PBLK),
    ):
        gathered[z, core, pl.ds(row, HD), pl.ds(pl.multiple_of(mine_lane + lane, 128), width)] = (
            ref[pl.ds(mine, HD), :]
        )

    def quarter(slot, part, kv):
        lane = pl.multiple_of(part * PART, 128)
        row = pl.multiple_of(kv * HD, 32)
        return gathered.at[slot, core, pl.ds(row, HD), pl.ds(lane, PART)]

    def ring(direction, slot, part, kv, index, device):
        ref = quarter(slot, part, kv)
        return remote(
            ref, ref, ring_send.at[direction, index], ring_recv.at[direction, index], device
        )

    def twin_copy(slot, part):
        lane = pl.multiple_of(part * PART, 128)
        ref = gathered.at[slot, core, pl.ds(0, KV), pl.ds(lane, PART)]
        index = slot * 2 + part
        return remote(ref, ref, twin_send.at[index], twin_recv.at[index], sibling)

    def twin_arrival(slot, part):
        lane = pl.multiple_of(part * PART, 128)
        ref = gathered.at[slot, twin, pl.ds(0, KV), pl.ds(lane, PART)]
        index = slot * 2 + part
        return remote(ref, ref, twin_send.at[index], twin_recv.at[index], sibling)

    for kv in range(2):
        ring(0, z, xh, kv, 4 + kv, up).start()
        ring(1, z, xh, kv, 4 + kv, down).start()
    twin_copy(z, xh).start()

    ones = jnp.ones((16, LANES), jnp.bfloat16)
    for slot in range(NZ):
        for cc in range(2):
            gathered[slot, cc, pl.ds(KV, 16), :] = ones

    wide = (ROWS, 128)
    lane_ids = lax.broadcasted_iota(jnp.int32, (128, 128), 1)
    row_ids = lax.broadcasted_iota(jnp.int32, (128, 128), 0)
    for half in range(2):
        source = z * 4 + half * 2 + core
        for piece in range(2):
            row = pos_ref[pl.ds(source * 2 + piece, 1), :]
            spread = jnp.where(lane_ids == row_ids, jnp.broadcast_to(row, (128, 128)), 0)
            column = jnp.sum(spread.astype(jnp.float32), axis=1, keepdims=True)
            column = jnp.broadcast_to(column.astype(jnp.int32), (128, 128))
            q_pos[pl.ds(half * ROWS + piece * 128, 128), :] = column
    position = q_pos[...]
    start = jnp.zeros_like(position)
    group = jnp.full_like(position, group_ref[0])
    end = jnp.int32(0)
    for r in range(15):
        end = end + lens_ref[r]
        past = position >= end
        start = jnp.where(past, end, start)
        group = jnp.where(past, group_ref[r + 1], group)
    q_start[...] = start
    q_grp[...] = group
    top[...] = jnp.full_like(top, NEG)
    accum[...] = jnp.zeros_like(accum)
    cache[...] = jnp.zeros_like(cache)
    own_q = pl.multiple_of(xh * ROWS, ROWS)
    other_q = pl.multiple_of(other * ROWS, ROWS)
    q_rows[pl.ds(own_q, ROWS), :] = jnp.transpose(
        q_ref[pl.ds(mine, HD), :].astype(jnp.float32)
    ).astype(jnp.bfloat16)

    for copy in exchange[:4]:
        copy.wait_recv()
    for kv in range(2):
        ring(0, z, other, kv, 6 + kv, up).start()
        ring(1, z, other, kv, 6 + kv, down).start()
    twin_copy(z, other).start()
    exchange[4].wait_recv()
    q_rows[pl.ds(other_q, ROWS), :] = jnp.transpose(q_other[...].astype(jnp.float32)).astype(
        jnp.bfloat16
    )

    packed = lax.broadcasted_iota(jnp.int32, (ROWS, 128), 0) + (z * 4 + core) * ROWS

    def unit(slot, cc):
        def tile(step, carry):
            rows = pl.ds(pl.multiple_of(step * TQ, TQ), TQ)
            queries = q_rows[rows, :]
            scores = jnp.dot(
                queries, gathered[slot, cc, pl.ds(0, HD), :], preferred_element_type=jnp.float32
            )
            position = q_pos[rows, :]
            start = q_start[rows, :]
            group = q_grp[rows, :]
            pieces = []
            for part in range(2):
                source = slot * 4 + part * 2 + cc
                for piece in range(2):
                    at = part * PART + piece * 128
                    keys = pos_ref[pl.ds(source * 2 + piece, 1), :]
                    seen = (keys <= position) & (keys >= start)
                    pieces.append(jnp.where(seen, scores[:, at : at + 128], NEG))
                at = part * PART + ROWS
                pieces.append(
                    jnp.where(group == owner_ref[source], scores[:, at : at + 128], NEG)
                )
            scores = jnp.concatenate(pieces, axis=1)
            before = top[rows, :]
            fresh = jnp.maximum(before, jnp.max(scores, axis=1, keepdims=True))
            weights = jnp.exp2((scores - jnp.tile(fresh, (1, LANES // 128))) * COEF)
            factor = jnp.exp2((before - fresh) * COEF)
            top[rows, :] = fresh
            added = lax.dot_general(
                weights.astype(jnp.bfloat16),
                gathered[slot, cc, pl.ds(HD, HD + 16), :],
                NT,
                preferred_element_type=jnp.float32,
            )
            accum[rows, :] = accum[rows, :] * factor[:, :1] + added
            return carry

        lax.fori_loop(0, QN // TQ, tile, 0)

        for half in range(2):
            for part in range(2):
                source = slot * 4 + part * 2 + cc
                hot = [
                    jnp.where(
                        pos_ref[pl.ds(source * 2 + piece, 1), :] == packed + half * 2 * ROWS,
                        1.0,
                        0.0,
                    ).astype(jnp.bfloat16)
                    for piece in range(2)
                ]
                cache[half] += lax.dot_general(
                    gathered[slot, cc, pl.ds(0, KV), pl.ds(part * PART, ROWS)],
                    jnp.concatenate(hot, axis=1),
                    NT,
                    preferred_element_type=jnp.float32,
                )

    def slot_of(k, direction):
        return lax.rem(z + jnp.where(direction == 0, NZ - k, k), NZ)

    def step(t, carry):
        k = t // 4 + 1
        i = t % 4
        below = lax.rem(z + NZ - k, NZ)
        above = lax.rem(z + k, NZ)
        first = i < 2
        part = jnp.where(first, xh, other)
        kv = i % 2
        index = k * 4 + i

        @pl.when(k < 4)
        def _():
            ring(0, below, part, kv, index, up).wait_recv()

            @pl.when((k < 3) | first)
            def _():
                ring(0, below, part, kv, index + 4, up).start()

            ring(1, above, part, kv, index, down).wait_recv()

            @pl.when(k < 3)
            def _():
                ring(1, above, part, kv, index + 4, down).start()

            @pl.when((k == 3) & (i >= 2))
            def _():
                ring(1, above, part, kv, index + 2, down).start()

            @pl.when(kv == 1)
            def _():
                twin_copy(below, part).start()
                twin_copy(above, part).start()

        @pl.when((k == 4) & first)
        def _():
            ring(0, below, xh, kv, index, up).wait_recv()
            ring(1, above, other, kv, index, down).wait_recv()

            @pl.when(kv == 1)
            def _():
                twin_copy(below, xh).start()
                twin_copy(below, other).start()

        @pl.when((k > 1) | first)
        def _():
            direction = i // 2
            from_twin = i % 2
            slot = slot_of(k - 1, direction)

            @pl.when(from_twin == 1)
            def _():
                twin_arrival(slot, 0).wait_recv()
                twin_arrival(slot, 1).wait_recv()

            unit(slot, jnp.where(from_twin == 1, twin, core))

        return carry

    lax.fori_loop(0, 16, step, 0)

    def last(from_twin, carry):
        slot = lax.rem(z + 4, NZ)

        @pl.when(from_twin == 1)
        def _():
            twin_arrival(slot, 0).wait_recv()
            twin_arrival(slot, 1).wait_recv()

        unit(slot, jnp.where(from_twin == 1, twin, core))
        return carry

    lax.fori_loop(0, 2, last, 0)

    def finished(at):
        block = accum[pl.ds(at, ROWS), :]
        scaled = block[:, :HD] / block[:, HD : HD + 1]
        return jnp.transpose(scaled).astype(jnp.bfloat16)

    att_send[...] = finished(other_q)
    result = [remote(att_send, att_recv, pair_send.at[5], pair_recv.at[5], pair)]
    result[0].start()
    for i in range(2):
        cache_send[i] = cache[other, pl.ds(i * HD, HD), :].astype(jnp.bfloat16)
        copy = remote(
            cache_send.at[i], cache_recv.at[i], pair_send.at[6 + i], pair_recv.at[6 + i], pair
        )
        copy.start()
        result.append(copy)
    att_ref[pl.ds(mine, HD), :] = finished(own_q)
    ck_ref[pl.ds(mine, HD), :] = cache[xh, pl.ds(0, HD), :].astype(jnp.bfloat16)
    cv_ref[pl.ds(mine, HD), :] = cache[xh, pl.ds(HD, HD), :].astype(jnp.bfloat16)
    result[0].wait_recv()
    att_ref[pl.ds(theirs, HD), :] = att_recv[...]
    result[1].wait_recv()
    ck_ref[pl.ds(theirs, HD), :] = cache_recv[0]
    result[2].wait_recv()
    cv_ref[pl.ds(theirs, HD), :] = cache_recv[1]

    for copy in exchange + result:
        copy.wait_send()

    def drain(index, carry):
        @pl.when(index < 14)
        def _():
            for direction in range(2):
                ring(direction, z, 0, 0, index + 4, up).wait_send()

        twin_copy(index // 2, index % 2).wait_send()
        return carry

    lax.fori_loop(0, 16, drain, 0)


def attend(query, keys, values, prefix_keys, prefix_values, lens, group, placement, owner):
    vmem = pl.BlockSpec(memory_space=pltpu.VMEM)
    smem = pl.BlockSpec(memory_space=pltpu.SMEM)
    shape = jax.ShapeDtypeStruct((KV, ROWS), jnp.bfloat16)
    dma = pltpu.SemaphoreType.DMA
    return pl.pallas_call(
        attention_kernel,
        out_shape=(shape, shape, shape),
        in_specs=[smem, smem, smem] + [vmem] * 6,
        out_specs=(vmem, vmem, vmem),
        scratch_shapes=[
            pltpu.VMEM((NZ, 2, AUG, LANES), jnp.bfloat16),
            pltpu.VMEM((HD, ROWS), jnp.bfloat16),
            pltpu.VMEM((QN, HD), jnp.bfloat16),
            pltpu.VMEM((QN, 128), jnp.int32),
            pltpu.VMEM((QN, 128), jnp.int32),
            pltpu.VMEM((QN, 128), jnp.int32),
            pltpu.VMEM((QN, 128), jnp.float32),
            pltpu.VMEM((QN, HD + 16), jnp.float32),
            pltpu.VMEM((2, KV, ROWS), jnp.float32),
            pltpu.VMEM((HD, ROWS), jnp.bfloat16),
            pltpu.VMEM((2, HD, ROWS), jnp.bfloat16),
            pltpu.VMEM((HD, ROWS), jnp.bfloat16),
            pltpu.VMEM((2, HD, ROWS), jnp.bfloat16),
            dma((2, 18)),
            dma((2, 18)),
            dma((16,)),
            dma((16,)),
            dma((8,)),
            dma((8,)),
        ],
        compiler_params=pltpu.CompilerParams(
            collective_id=0, has_side_effects=True, vmem_limit_bytes=48 * 1024 * 1024
        ),
    )(
        lens,
        group,
        owner,
        placement.reshape(64, 128),
        query.T,
        keys.T,
        values.T,
        prefix_keys.T,
        prefix_values.T,
    )


def shards(
    query,
    keys,
    values,
    prefix_keys,
    prefix_values,
    residual,
    out_weight,
    suffix_lens,
    req_group,
    placement,
    prefix_owner,
):
    attended, cache_keys, cache_values = attend(
        query,
        keys,
        values,
        prefix_keys,
        prefix_values,
        suffix_lens,
        req_group,
        placement,
        prefix_owner,
    )
    term = jnp.dot(attended.T, out_weight, preferred_element_type=jnp.float32)
    summed = lax.psum_scatter(
        term.astype(jnp.bfloat16), "tp", scatter_dimension=1, tiled=True
    ).astype(jnp.float32)
    hidden = (residual.astype(jnp.float32) + summed).astype(jnp.bfloat16)
    return (hidden, cache_keys.T, cache_values.T)


def solution(mesh):
    return jax.shard_map(
        shards,
        mesh=mesh,
        in_specs=(
            P("seq", "tp"),
            P("seq", "tp"),
            P("seq", "tp"),
            P("seq", "tp"),
            P("seq", "tp"),
            P("seq", "tp"),
            P("tp", None),
            P(),
            P(),
            P(),
            P(),
        ),
        out_specs=(P("seq", "tp"), P("seq", "tp"), P("seq", "tp")),
        check_vma=False,
    )
```

time: 509 us -> 152 us (0.30)
  the two profiles are of different devices: /device:TPU:1 before, /device:TPU:4 now
where the time goes in v1:
time: 152 us; the launch traced here: 151 us
  Pallas kernels  78.6 us (52%)
  waiting for transfers between devices  43.5 us (29%)
  between operations  14.1 us (9%)
  local copies, waits for them, and re-layouts  10.5 us (7%)
  matrix products  2.8 us (2%)
  other arithmetic  1.79 us (1%)
    pallas_call x1, Pallas kernels, attend(): pl.pallas_call(attention_kernel, out_shape=(shape, shape, shape), in_spec...  78.6 us
    reduce_scatter x1, waiting for transfers between devices, shards(): lax.psum_scatter(term.astype(jnp.bfloat16), 'tp', scatter_dimension=1, ti...  43.5 us
    unnamed x24, local copies, waits for them, and re-layouts  10.5 us
  transfers between devices with their start and end apart: 1, of which 1 were waited for; matrix products, arithmetic and copies ran while one was open for 0% of the time, Pallas kernels for 0%

profile of v1, /device:TPU:4, one launch (start us, length us, event | category | flops | bytes accessed | tf_op | source)
XLA Modules:
  0.0 151.3 jit_solution(10056274586717184897)
XLA Ops:
  7.2 0.0 copy-start
  7.2 0.0 reduce-scatter.2.cloned.1.call-start
  7.2 0.0 copy-start.2
  7.2 1.1 copy-done.2
  8.3 0.9 copy-done.3
  9.3 0.0 copy-start.4
  9.3 0.9 copy-done.4
  10.2 0.0 copy-start.5
  10.2 0.9 copy-done.5
  11.1 0.9 copy-done.6
  12.0 0.8 copy-done.7
  12.8 0.7 copy-done.8
  13.4 0.7 copy-done.9
  14.1 0.7 copy-done.10
  14.7 78.6 %shard_map.130 = (bf16[448,256]{1,0:T(8,128)(2,1)S(1)}, bf16[448,256]{1,0:T(8,128)(2,1)S(1)}, bf16[448,256]{1,0:T(8,128)(2,1)S(1)}) custom-call(s32[16]{0:T(128)S(1)} %copy-done.8, s32[16]{0:T(128)S(1)} %copy-done.9, s32[32]{0:T(128)S(1)} %copy-done.10, s32[64,128]{1,0:T(8,128)S(1)} %bitcast.17, bf16[448,256]{1,0:T(8,128)(2,1)S(1)} %bitcast.12, ...), custom_call_target="tpu_custom_call" | custom-call | tf_op jit(solution)/shard_map/pallas_call | solution.py:388
  93.3 0.0 copy-start.1
  93.3 0.7 copy-done.1
  94.0 0.0 copy-done
  94.0 2.8 %convolution_convert_fusion = bf16[256,3584]{0,1:T(8,128)(2,1)} fusion(bf16[448,256]{1,0:T(8,128)(2,1)S(1)} %get-tuple-element.6, bf16[448,3584]{1,0:T(8,128)(2,1)S(1)} %copy-done), kind=kOutput, calls=%fused_computation | convolution fusion | flops 823001088 | bytes 5275648 | tf_op jit(solution)/shard_map/dot_general | solution.py:454
  96.8 0.0 reduce-scatter.2.cloned.1.call-update
  96.9 43.5 %reduce-scatter.2.cloned.1.call-done = bf16[256,448]{0,1:T(8,128)(2,1)} async-done(((bf16[256,3584]{0,1:T(8,128)(2,1)}), bf16[256,448]{0,1:T(8,128)(2,1)}) %reduce-scatter.2.cloned.1.call-update) | async-done | bytes 229392 | tf_op jit(solution)/shard_map/reduce_scatter | solution.py:455
  140.3 1.8 %add_convert_fusion = bf16[256,448]{0,1:T(8,128)(2,1)} fusion(bf16[256,448]{0,1:T(8,128)(2,1)} %reduce-scatter.2.cloned.1.call-done, bf16[256,448]{0,1:T(8,128)(2,1)} %param.16), kind=kLoop, calls=%fused_computation.1 | loop fusion | flops 458752 | bytes 688128 | tf_op jit(solution)/shard_map/convert_element_type | solution.py:458
  142.1 1.6 %copy.16 = bf16[256,448]{0,1:T(8,128)(2,1)} copy(bf16[256,448]{0,1:T(8,128)(2,1)} %bitcast.11) | data formatting | bytes 458752
  143.8 0.7 copy.17
  (6 shorter events, 0.0 us)
Async XLA Ops:
  7.2 86.9 %copy-start = (bf16[448,3584]{1,0:T(8,128)(2,1)S(1)}, bf16[448,3584]{1,0:T(8,128)(2,1)}, u32[]{:S(2)}) copy-start(bf16[448,3584]{1,0:T(8,128)(2,1)} %param.17) | copy-start | bytes 9633796
  7.2 133.2 %reduce-scatter.2.cloned.1.call-start = ((), (), s32[]{:S(2)}) async-start(), calls=%async_computation.1 | async-start | bytes 2064384 | tf_op jit(solution)/shard_map/reduce_scatter | solution.py:455
  7.2 1.1 copy-start.2
  8.3 0.9 copy-start.3
  9.3 0.9 copy-start.4
  10.2 0.9 copy-start.5
  11.1 0.9 copy-start.6
  12.0 0.8 copy-start.7
  12.8 0.7 copy-start.8
  13.4 0.7 copy-start.9
  14.1 0.7 copy-start.10
  93.3 0.7 copy-start.1
Sparse Core Ops, SparseCore 0:
  97.0 43.3 reduce-scatter.1

commit v2 on v0

v2 whole, which is shorter than its diff:
```python
import functools
import math

import jax
import jax.numpy as jnp
from jax import lax
from jax.experimental import pallas as pl
from jax.experimental.pallas import tpu as pltpu
from jax.sharding import PartitionSpec as P

HD = 224
HALF = HD // 2
ROWS = 256
PBLK = 128
PART = ROWS + PBLK
LANES = 2 * PART
QN = 2 * ROWS
KV = 2 * HD
NZ = 8
TP = 8
D = 3584
TQ = 256
NEG = -1e30
COEF = math.log2(math.e) / math.sqrt(HD)
MESH = pl.DeviceIdType.MESH
NT = (((1,), (1,)), ((), ()))
BF = jnp.bfloat16
F32 = jnp.float32


def dot(a, b):
    return jnp.dot(a, b, preferred_element_type=F32)


def dot_nt(a, b):
    return lax.dot_general(a, b, NT, preferred_element_type=F32)


def step_kernel(
    lens_hbm,
    group_hbm,
    owner_hbm,
    pos_hbm,
    q_hbm,
    k_hbm,
    v_hbm,
    pk_hbm,
    pv_hbm,
    res_hbm,
    w_hbm,
    hid_ref,
    ck_ref,
    cv_ref,
    lens_ref,
    group_ref,
    owner_ref,
    pos_ref,
    res_ref,
    w_ref,
    q_own,
    q_other,
    keys,
    vals0,
    vals1,
    weights_ref,
    hot_ref,
    tops,
    q_rows,
    q_pos,
    q_start,
    q_grp,
    top,
    accum,
    cache_k,
    cache_v,
    swap_out,
    swap_in,
    w_send,
    w_all,
    att_out,
    att_all,
    projected,
    local_sem,
    ring_send,
    ring_recv,
    twin_send,
    twin_recv,
    pair_send,
    pair_recv,
    w_send_sem,
    w_recv_sem,
    w_twin_send,
    w_twin_recv,
    att_send_sem,
    att_recv_sem,
):
    seq = lax.axis_index("seq")
    tp = lax.axis_index("tp")
    z = seq // 4
    xh = (seq // 2) % 2
    core = seq % 2
    other = 1 - xh
    twin = 1 - core

    def dev(zz, xx, cc, tt):
        return (zz * 4 + xx * 2 + cc, tt)

    up = dev(lax.rem(z + 1, NZ), xh, core, tp)
    down = dev(lax.rem(z + NZ - 1, NZ), xh, core, tp)
    pair = dev(z, other, core, tp)
    sibling = dev(z, xh, twin, tp)

    def plane(e):
        return lax.rem(xh + e // TP, 2), lax.rem(tp + e, TP)

    mine = pl.multiple_of(xh * HD, 32)
    theirs = pl.multiple_of(other * HD, 32)
    mine_lane = pl.multiple_of(xh * PART, 128)

    blocks = (keys, vals0, vals1)
    heights = (HD, HALF, HALF)
    offsets = (0, 0, HALF)
    suffix = (k_hbm, v_hbm, v_hbm)
    prefix = (pk_hbm, pv_hbm, pv_hbm)

    def landing(f, lane, width):
        at = pl.multiple_of(mine_lane + lane, 128)
        return blocks[f].at[z, core, pl.ds(0, heights[f]), pl.ds(at, width)]

    def rows_of(ref, f, base):
        return ref.at[pl.ds(pl.multiple_of(base + offsets[f], 16), heights[f])]

    own = []
    for f in range(3):
        own.append(
            (
                pltpu.make_async_copy(
                    rows_of(suffix[f], f, mine), landing(f, 0, ROWS), local_sem.at[2 * f]
                ),
                pltpu.make_async_copy(
                    rows_of(prefix[f], f, mine), landing(f, ROWS, PBLK), local_sem.at[2 * f + 1]
                ),
            )
        )
    small = [
        pltpu.make_async_copy(src, dst, local_sem.at[6 + i])
        for i, (src, dst) in enumerate(
            (
                (lens_hbm, lens_ref),
                (group_hbm, group_ref),
                (owner_hbm, owner_ref),
                (pos_hbm, pos_ref),
                (q_hbm.at[pl.ds(mine, HD)], q_own),
                (w_hbm.at[pl.ds(pl.multiple_of(core * HD, 32), HD)], w_ref),
                (res_hbm, res_ref),
            )
        )
    ]
    for copy in own[0] + own[1]:
        copy.start()
    for copy in small[:5]:
        copy.start()
    for copy in own[2]:
        copy.start()
    for copy in small[5:]:
        copy.start()

    barrier = pltpu.get_barrier_semaphore()
    for peer in (up, down, sibling):
        pl.semaphore_signal(barrier, inc=1, device_id=peer, device_id_type=MESH)

    def greet(e, carry):
        xx, tt = plane(e)
        pl.semaphore_signal(barrier, inc=1, device_id=dev(z, xx, core, tt), device_id_type=MESH)
        return carry

    lax.fori_loop(1, 2 * TP, greet, 0)
    pl.semaphore_wait(barrier, 2 * TP + 2)

    def remote(src, dst, send, recv, device):
        return pltpu.make_async_remote_copy(
            src_ref=src,
            dst_ref=dst,
            send_sem=send,
            recv_sem=recv,
            device_id=device,
            device_id_type=MESH,
        )

    def pair_copy(src, dst, i):
        return remote(src, dst, pair_send.at[i], pair_recv.at[i], pair)

    exchange = [
        (
            pair_copy(rows_of(suffix[f], f, theirs), landing(f, 0, ROWS), 2 * f),
            pair_copy(rows_of(prefix[f], f, theirs), landing(f, ROWS, PBLK), 2 * f + 1),
        )
        for f in range(3)
    ]
    exchange_q = pair_copy(q_hbm.at[pl.ds(theirs, HD)], q_other, 6)

    def block(f, slot, cc, part):
        lane = pl.multiple_of(part * PART, 128)
        return blocks[f].at[slot, cc, pl.ds(0, heights[f]), pl.ds(lane, PART)]

    def ring(f, direction, slot, part, n):
        ref = block(f, slot, core, part)
        index = f * 8 + n
        return remote(
            ref,
            ref,
            ring_send.at[direction, index],
            ring_recv.at[direction, index],
            down if direction else up,
        )

    def twin_copy(f, slot, part, cc):
        ref = block(f, slot, cc, part)
        index = f * 16 + slot * 2 + part
        return remote(ref, ref, twin_send.at[index], twin_recv.at[index], sibling)

    def send_own(f, part, n):
        ring(f, 0, z, part, n).start()
        ring(f, 1, z, part, n).start()
        twin_copy(f, z, part, core).start()

    for copy in exchange[0]:
        copy.start()
    for copy in own[0]:
        copy.wait()
    send_own(0, xh, 0)
    exchange_q.start()
    for f in (1, 2):
        for copy in exchange[f]:
            copy.start()
    for copy in own[1]:
        copy.wait()
    send_own(1, xh, 0)

    for copy in small[:5]:
        copy.wait()
    lane_ids = lax.broadcasted_iota(jnp.int32, (128, 128), 1)
    row_ids = lax.broadcasted_iota(jnp.int32, (128, 128), 0)
    for half in range(2):
        source = z * 4 + half * 2 + core
        for piece in range(2):
            row = pos_ref[pl.ds(source * 2 + piece, 1), :]
            spread = jnp.where(lane_ids == row_ids, jnp.broadcast_to(row, (128, 128)), 0)
            column = jnp.sum(spread.astype(F32), axis=1, keepdims=True)
            q_pos[pl.ds(half * ROWS + piece * 128, 128), :] = jnp.broadcast_to(
                column.astype(jnp.int32), (128, 128)
            )
    position = q_pos[...]
    start = jnp.zeros_like(position)
    group = jnp.full_like(position, group_ref[0])
    end = jnp.int32(0)
    for r in range(15):
        end = end + lens_ref[r]
        past = position >= end
        start = jnp.where(past, end, start)
        group = jnp.where(past, group_ref[r + 1], group)
    q_start[...] = start
    q_grp[...] = group
    own_q = pl.multiple_of(xh * ROWS, ROWS)
    other_q = pl.multiple_of(other * ROWS, ROWS)
    q_rows[pl.ds(own_q, ROWS), :] = jnp.transpose(q_own[...].astype(F32)).astype(BF)

    for copy in exchange[0]:
        copy.wait_recv()
    send_own(0, other, 1)
    top[...] = jnp.full_like(top, NEG)
    accum[...] = jnp.zeros_like(accum)
    cache_k[...] = jnp.zeros_like(cache_k)
    cache_v[...] = jnp.zeros_like(cache_v)
    ones = jnp.ones((16, LANES), BF)
    for slot in range(NZ):
        for cc in range(2):
            vals0[slot, cc, pl.ds(HALF, 16), :] = ones
    exchange_q.wait_recv()
    q_rows[pl.ds(other_q, ROWS), :] = jnp.transpose(q_other[...].astype(F32)).astype(BF)

    packed = lax.broadcasted_iota(jnp.int32, (ROWS, 128), 0) + (z * 4 + core) * ROWS

    def slot_at(u):
        k = (u + 1) // 2
        return lax.rem(z + jnp.where(u % 2 == 1, NZ - k, k), NZ)

    def arrived(f, slot):
        for part in range(2):
            twin_copy(f, slot, part, twin).wait_recv()

    def each_unit(f, lo, hi, body):
        def visit(i, carry):
            u = i // 2
            from_twin = i % 2
            slot = slot_at(u)

            @pl.when(from_twin == 1)
            def _():
                arrived(f, slot)

            cc = jnp.where(from_twin == 1, twin, core)
            body(slot, cc, slot * 2 + cc)
            return carry

        lax.fori_loop(lo * 2, hi * 2, visit, 0)

    def score_unit(slot, cc, unit):
        def tile(step, carry):
            rows = pl.ds(pl.multiple_of(step * TQ, TQ), TQ)
            scores = dot(q_rows[rows, :], keys[slot, cc])
            position = q_pos[rows, :]
            start = q_start[rows, :]
            group = q_grp[rows, :]
            pieces = []
            for part in range(2):
                source = slot * 4 + part * 2 + cc
                for piece in range(2):
                    at = part * PART + piece * 128
                    where = pos_ref[pl.ds(source * 2 + piece, 1), :]
                    seen = (where <= position) & (where >= start)
                    pieces.append(jnp.where(seen, scores[:, at : at + 128], NEG))
                at = part * PART + ROWS
                pieces.append(
                    jnp.where(group == owner_ref[source], scores[:, at : at + 128], NEG)
                )
            scores = jnp.concatenate(pieces, axis=1)
            fresh = jnp.maximum(top[rows, :], jnp.max(scores, axis=1, keepdims=True))
            top[rows, :] = fresh
            tops[unit, rows, :] = fresh
            weights_ref[unit, rows, :] = jnp.exp2(
                (scores - jnp.tile(fresh, (1, LANES // 128))) * COEF
            ).astype(BF)
            return carry

        lax.fori_loop(0, QN // TQ, tile, 0)

        for part in range(2):
            source = slot * 4 + part * 2 + cc
            for half in range(2):
                hot = [
                    jnp.where(
                        pos_ref[pl.ds(source * 2 + piece, 1), :] == packed + half * 2 * ROWS,
                        1.0,
                        0.0,
                    ).astype(BF)
                    for piece in range(2)
                ]
                hot_ref[unit, pl.ds(half * ROWS, ROWS), pl.ds(part * ROWS, ROWS)] = (
                    jnp.concatenate(hot, axis=1)
                )
        cache_k[...] += moved(keys, HD, slot, cc, unit)

    def moved(ref, height, slot, cc, unit):
        total = None
        for part in range(2):
            term = dot_nt(
                ref[slot, cc, pl.ds(0, height), pl.ds(part * PART, ROWS)],
                hot_ref[unit, :, pl.ds(part * ROWS, ROWS)],
            )
            total = term if total is None else total + term
        return total

    def value_unit(f, slot, cc, unit):
        ref = blocks[f]
        which = f - 1
        factor = jnp.exp2((tops[unit, :, pl.ds(0, 128)] - top[...]) * COEF)
        width = ref.shape[2]
        added = dot_nt(weights_ref[unit], ref[slot, cc])
        accum[which, :, pl.ds(0, width)] = (
            accum[which, :, pl.ds(0, width)] + added * factor[:, :width]
        )
        cache_v[which] = cache_v[which] + moved(ref, HALF, slot, cc, unit)

    def service(f, n):
        k = n // 2 + 1
        below = lax.rem(z + NZ - k, NZ)
        above = lax.rem(z + k, NZ)
        even = n % 2 == 0
        part = jnp.where(even, xh, other)
        part_above = jnp.where(n == 6, other, part)
        ring(f, 0, below, part, n).wait_recv()

        @pl.when(n < 5)
        def _():
            ring(f, 0, below, part, n + 2).start()

        ring(f, 1, above, part_above, n).wait_recv()

        @pl.when((n < 4) | (n == 5))
        def _():
            ring(f, 1, above, part, n + 2 - n // 5).start()

        twin_copy(f, below, part, core).start()
        twin_copy(f, above, part_above, core).start()

    def prepare_weights():
        small[5].wait()
        for t in range(TP):
            for half in range(2):
                w_send[t, :, pl.ds(half * 128, HALF)] = jnp.transpose(
                    w_ref[pl.ds(half * HALF, HALF), pl.ds(t * KV, KV)].astype(F32)
                ).astype(BF)

        def send(e, carry):
            w_copy(e).start()
            return carry

        lax.fori_loop(1, TP, send, 0)
        w_all[2 * tp + core] = w_send[tp]
        w_twin(0, core).start()

    def w_copy(e):
        to = lax.rem(tp + e, TP)
        return remote(
            w_send.at[to],
            w_all.at[2 * tp + core],
            w_send_sem.at[e],
            w_recv_sem.at[e],
            dev(z, xh, core, to),
        )

    def w_arrival(e):
        head = 2 * lax.rem(tp + TP - e, TP) + core
        return remote(
            w_all.at[head], w_all.at[head], w_send_sem.at[e], w_recv_sem.at[e], sibling
        )

    def w_twin(e, cc):
        head = 2 * lax.rem(tp + TP - e, TP) + cc
        return remote(
            w_all.at[head], w_all.at[head], w_twin_send.at[e], w_twin_recv.at[e], sibling
        )

    def share_weights():
        def share(e, carry):
            w_arrival(e).wait_recv()
            w_twin(e, core).start()
            return carry

        lax.fori_loop(1, TP, share, 0)

    swaps = []

    def swap(i, index):
        height = HD if i == 0 else HALF
        base = (0, HD, HD + HALF)[i]
        rows = pl.ds(base, height)
        return pair_copy(swap_out.at[rows], swap_in.at[rows], 7 + i)

    def send_cache(i, ref):
        height = HD if i == 0 else HALF
        base = (0, HD, HD + HALF)[i]
        out = ck_ref if i == 0 else cv_ref
        offset = (0, 0, HALF)[i]

        @pl.when(xh == 0)
        def _():
            swap_out[pl.ds(base, height), :] = ref[:, ROWS:].astype(BF)
            out[pl.ds(offset, height), :] = ref[:, :ROWS].astype(BF)

        @pl.when(xh == 1)
        def _():
            swap_out[pl.ds(base, height), :] = ref[:, :ROWS].astype(BF)
            out[pl.ds(HD + offset, height), :] = ref[:, ROWS:].astype(BF)

        swap(i, 0).start()

    def att_copy(half, e):
        xx, tt = plane(e)
        return remote(
            att_out.at[half, xx],
            att_all.at[half, 2 * tp + xh],
            att_send_sem.at[half * 16 + e],
            att_recv_sem.at[half * 16 + e],
            dev(z, xx, core, tt),
        )

    def att_head(e):
        return 2 * lax.rem(tp + 2 * TP - e, TP) + lax.rem(xh + e // TP, 2)

    def att_arrival(half, e):
        head = att_head(e)
        return remote(
            att_all.at[half, head],
            att_all.at[half, head],
            att_send_sem.at[half * 16 + e],
            att_recv_sem.at[half * 16 + e],
            sibling,
        )

    def finish(half):
        scaled = accum[half, :, pl.ds(0, HALF)] / accum[0, :, pl.ds(HALF, 1)]
        turned = jnp.transpose(scaled).astype(BF)
        att_out[half, 0] = turned[:, :ROWS]
        att_out[half, 1] = turned[:, ROWS:]

        def send(e, carry):
            att_copy(half, e).start()
            return carry

        lax.fori_loop(1, 2 * TP, send, 0)
        att_all[half, 2 * tp + xh] = att_out[half, xh]

    def project(half):
        def add(e, carry):
            @pl.when(e > 0)
            def _():
                att_arrival(half, e).wait_recv()

            head = att_head(e)
            projected[...] += dot(
                w_all[head, :, pl.ds(half * 128, HALF)], att_all[half, head]
            )
            return carry

        lax.fori_loop(0, 2 * TP, add, 0)

    def key_step(n, carry):
        service(0, n)

        @pl.when(n == 1)
        def _():
            prepare_weights()

        @pl.when(n == 5)
        def _():
            for copy in exchange[1]:
                copy.wait_recv()
            send_own(1, other, 1)

        lo = jnp.where(n == 0, 0, jnp.maximum(n - 1, 1))
        each_unit(0, lo, jnp.maximum(n, 1), score_unit)
        return carry

    lax.fori_loop(0, 7, key_step, 0)

    def first_step(n, carry):
        service(1, n)

        @pl.when(n == 2)
        def _():
            send_cache(0, cache_k)
            share_weights()

        @pl.when(n == 5)
        def _():
            for copy in own[2]:
                copy.wait()
            send_own(2, xh, 0)
            for copy in exchange[2]:
                copy.wait_recv()
            send_own(2, other, 1)

        @pl.when(n < 2)
        def _():
            each_unit(0, n + 6, n + 7, score_unit)

        @pl.when(n >= 2)
        def _():
            each_unit(1, n - 2, n - 1, functools.partial(value_unit, 1))

        return carry

    lax.fori_loop(0, 7, first_step, 0)

    def second_step(n, carry):
        service(2, n)

        @pl.when(n < 2)
        def _():
            each_unit(1, 5 + 2 * n, 7 + n, functools.partial(value_unit, 1))

        @pl.when(n == 1)
        def _():
            finish(0)
            send_cache(1, cache_v.at[0])

        lo = jnp.where(n < 3, 0, 2 * n - 5)
        hi = jnp.where(n == 6, 7, jnp.where(n < 2, 0, 2 * n - 3))
        each_unit(2, lo, hi, functools.partial(value_unit, 2))
        return carry

    lax.fori_loop(0, 7, second_step, 0)
    each_unit(2, 7, 8, functools.partial(value_unit, 2))
    finish(1)
    send_cache(2, cache_v.at[1])

    for e in range(TP):
        w_twin(e, twin).wait_recv()
    small[6].wait()
    projected[...] = res_ref[...].astype(F32)
    project(0)
    for i in range(3):
        swap(i, 0).wait_recv()
    for i, out in enumerate((ck_ref, cv_ref, cv_ref)):
        height = HD if i == 0 else HALF
        base = (0, HD, HD + HALF)[i]
        offset = (0, 0, HALF)[i]
        out[pl.ds(pl.multiple_of(theirs + offset, 16), height), :] = swap_in[
            pl.ds(base, height), :
        ]
    project(1)
    hid_ref[...] = projected[...].astype(BF)

    for f in range(3):
        for copy in exchange[f]:
            copy.wait_send()
        swap(f, 0).wait_send()

        def drain(n, carry, f=f):
            ring(f, 0, z, 0, n).wait_send()
            ring(f, 1, z, 0, n).wait_send()
            return carry

        lax.fori_loop(0, 7, drain, 0)

        def drain_twin(n, carry, f=f):
            twin_copy(f, n // 2, n % 2, core).wait_send()
            return carry

        lax.fori_loop(0, 16, drain_twin, 0)
    exchange_q.wait_send()

    def drain_weights(e, carry):
        @pl.when(e > 0)
        def _():
            w_copy(e).wait_send()

        w_twin(e, core).wait_send()
        return carry

    lax.fori_loop(0, TP, drain_weights, 0)

    def drain_att(e, carry):
        att_copy(0, e).wait_send()
        att_copy(1, e).wait_send()
        return carry

    lax.fori_loop(1, 2 * TP, drain_att, 0)


def whole_step(*operands):
    vmem = pl.BlockSpec(memory_space=pltpu.VMEM)
    hbm = pl.BlockSpec(memory_space=pl.ANY)
    shape = jax.ShapeDtypeStruct((KV, ROWS), BF)
    dma = pltpu.SemaphoreType.DMA
    buffer = pltpu.VMEM
    return pl.pallas_call(
        step_kernel,
        out_shape=(shape, shape, shape),
        in_specs=[hbm] * 11,
        out_specs=(vmem, vmem, vmem),
        scratch_shapes=[
            pltpu.SMEM((16,), jnp.int32),
            pltpu.SMEM((16,), jnp.int32),
            pltpu.SMEM((32,), jnp.int32),
            buffer((64, 128), jnp.int32),
            buffer((KV, ROWS), BF),
            buffer((HD, D), BF),
            buffer((HD, ROWS), BF),
            buffer((HD, ROWS), BF),
            buffer((NZ, 2, HD, LANES), BF),
            buffer((NZ, 2, HALF + 16, LANES), BF),
            buffer((NZ, 2, HALF, LANES), BF),
            buffer((2 * NZ, QN, LANES), BF),
            buffer((2 * NZ, QN, QN), BF),
            buffer((2 * NZ, QN, 128), F32),
            buffer((QN, HD), BF),
            buffer((QN, 128), jnp.int32),
            buffer((QN, 128), jnp.int32),
            buffer((QN, 128), jnp.int32),
            buffer((QN, 128), F32),
            buffer((2, QN, 128), F32),
            buffer((HD, QN), F32),
            buffer((2, HALF, QN), F32),
            buffer((KV, ROWS), BF),
            buffer((KV, ROWS), BF),
            buffer((TP, KV, 256), BF),
            buffer((2 * TP, KV, 256), BF),
            buffer((2, 2, HALF, ROWS), BF),
            buffer((2, 2 * TP, HALF, ROWS), BF),
            buffer((KV, ROWS), F32),
            dma((13,)),
            dma((2, 24)),
            dma((2, 24)),
            dma((48,)),
            dma((48,)),
            dma((10,)),
            dma((10,)),
            dma((TP,)),
            dma((TP,)),
            dma((TP,)),
            dma((TP,)),
            dma((32,)),
            dma((32,)),
        ],
        compiler_params=pltpu.CompilerParams(
            collective_id=0, has_side_effects=True, vmem_limit_bytes=60 * 1024 * 1024
        ),
    )(*operands)


def shards(
    query,
    keys,
    values,
    prefix_keys,
    prefix_values,
    residual,
    out_weight,
    suffix_lens,
    req_group,
    placement,
    prefix_owner,
):
    hidden, cache_keys, cache_values = whole_step(
        suffix_lens,
        req_group,
        prefix_owner,
        placement.reshape(64, 128),
        query.T,
        keys.T,
        values.T,
        prefix_keys.T,
        prefix_values.T,
        residual.T,
        out_weight,
    )
    return (hidden.T, cache_keys.T, cache_values.T)


def solution(mesh):
    return jax.shard_map(
        shards,
        mesh=mesh,
        in_specs=(
            P("seq", "tp"),
            P("seq", "tp"),
            P("seq", "tp"),
            P("seq", "tp"),
            P("seq", "tp"),
            P("seq", "tp"),
            P("tp", None),
            P(),
            P(),
            P(),
            P(),
        ),
        out_specs=(P("seq", "tp"), P("seq", "tp"), P("seq", "tp")),
        check_vma=False,
    )
```

time: 509 us -> 110 us (0.22)
  waiting for transfers between devices: 331 us -> 0 us
  Pallas kernels: 0 us -> 105 us
  local copies, waits for them, and re-layouts: 98 us -> 4.92 us
  matrix products: 43.9 us -> 0 us
  other arithmetic: 21 us -> 0 us
  between operations: 13.9 us -> 0.64 us
    all_gather x4 -> x0, waiting for transfers between devices: 329 us -> none  [the longest x1 94.4 us: shards(): lax.all_gather(values, 'seq', axis=0, tiled=True)]
    pallas_call x0 -> x1, Pallas kernels: none -> 105 us  [whole_step(): pl.pallas_call(step_kernel, out_shape=(shape, shape, shape), in_specs=[hb...]
    scatter x2 -> x0, local copies, waits for them, and re-layouts: 71.6 us -> none  [the longest x1 35.8 us: shards(): cache[0].at[target].set(pieces[0], mode='drop')]
    dot_general x5 -> x0, matrix products: 43.9 us -> none  [the longest x2 20.9 us: absorb(): jnp.einsum('hqk,khd->hqd', weights, value_heads, preferred_element_type=j...]
    all_gather x2 -> x0, local copies, waits for them, and re-layouts: 23.2 us -> none  [the longest x1 11.6 us: shards(): lax.all_gather(keys, 'seq', axis=0, tiled=True)]
    reduce_sum x6 -> x0, other arithmetic: 13.8 us -> none  [the longest x2 11.3 us: absorb(): total = factor * total + jnp.sum(weights.astype(jnp.float32), axis=2)]
  transfers between devices with their start and end apart: 5 -> 0, of which waited for: 4 -> 0; matrix products, arithmetic and copies ran while one was open for 29% -> 0% of each run, Pallas kernels for 0% -> 0%
where the time goes in v2:
time: 110 us
  Pallas kernels  105 us (95%)
  local copies, waits for them, and re-layouts  4.92 us (4%)
    pallas_call x1, Pallas kernels, whole_step(): pl.pallas_call(step_kernel, out_shape=(shape, shape, shape), in_specs=[hb...  105 us
    unnamed x3, local copies, waits for them, and re-layouts  4.92 us

profile of v2, /device:TPU:1, one launch (start us, length us, event | category | flops | bytes accessed | tf_op | source)
XLA Modules:
  0.0 110.3 jit_solution(5291552233316550657)
XLA Ops:
  0.6 104.8 %shard_map.130 = (bf16[448,256]{1,0:T(8,128)(2,1)}, bf16[448,256]{1,0:T(8,128)(2,1)}, bf16[448,256]{1,0:T(8,128)(2,1)}) custom-call(s32[16]{0:T(128)} %lens_hbm.1, s32[16]{0:T(128)} %group_hbm.1, s32[32]{0:T(128)} %owner_hbm.1, s32[64,128]{1,0:T(8,128)} %bitcast.19, bf16[448,256]{1,0:T(8,128)(2,1)} %bitcast.13, bf16[448,256]{1,0:T(8,128)(2,1)} %bitcast.14, ...), custom_call_target="tpu_custom_call" | custom-call | tf_op jit(solution)/shard_map/pallas_call | solution.py:649
  105.4 1.6 %copy.17 = bf16[256,448]{0,1:T(8,128)(2,1)} copy(bf16[256,448]{0,1:T(8,128)(2,1)} %bitcast.12) | data formatting | bytes 458752
  107.0 1.6 %copy.18 = bf16[256,448]{0,1:T(8,128)(2,1)} copy(bf16[256,448]{0,1:T(8,128)(2,1)} %bitcast.11) | data formatting | bytes 458752
  108.7 1.6 %copy.19 = bf16[256,448]{0,1:T(8,128)(2,1)} copy(bf16[256,448]{0,1:T(8,128)(2,1)} %bitcast.10) | data formatting | bytes 458752

commit v3 on v2

--- a/solution.py
+++ b/solution.py
@@ -48,9 +48,7 @@
     pv_hbm,
     res_hbm,
     w_hbm,
-    hid_ref,
-    ck_ref,
-    cv_ref,
+    out_ref,
     lens_ref,
     group_ref,
     owner_ref,
@@ -94,6 +92,7 @@
     att_send_sem,
     att_recv_sem,
 ):
+    hid_ref, ck_ref, cv_ref = (out_ref.at[pl.ds(i * KV, KV)] for i in range(3))
     seq = lax.axis_index("seq")
     tp = lax.axis_index("tp")
     z = seq // 4
@@ -516,34 +515,53 @@
 
         lax.fori_loop(0, 2 * TP, add, 0)
 
-    def key_step(n, carry):
-        service(0, n)
-
-        @pl.when(n == 1)
+    first_values = functools.partial(value_unit, 1)
+    second_values = functools.partial(value_unit, 2)
+
+    def round_a(i, carry):
+        service(0, i)
+
+        @pl.when(i == 1)
         def _():
             prepare_weights()
 
-        @pl.when(n == 5)
+        @pl.when(i == 3)
         def _():
             for copy in exchange[1]:
                 copy.wait_recv()
             send_own(1, other, 1)
 
-        lo = jnp.where(n == 0, 0, jnp.maximum(n - 1, 1))
-        each_unit(0, lo, jnp.maximum(n, 1), score_unit)
+        lo = jnp.where(i == 0, 0, jnp.maximum(i - 1, 1))
+        each_unit(0, lo, jnp.maximum(i, 1), score_unit)
         return carry
 
-    lax.fori_loop(0, 7, key_step, 0)
-
-    def first_step(n, carry):
-        service(1, n)
-
-        @pl.when(n == 2)
-        def _():
-            send_cache(0, cache_k)
+    lax.fori_loop(0, 4, round_a, 0)
+
+    def round_b(i, carry):
+        @pl.when(i < 2)
+        def _():
+            service(0, i + 4)
+
+        @pl.when(i >= 2)
+        def _():
+            service(1, i - 2)
+
+        each_unit(0, i + 3, i + 4, score_unit)
+        return carry
+
+    lax.fori_loop(0, 4, round_b, 0)
+
+    def round_c(i, carry):
+        @pl.when(i == 0)
+        def _():
+            service(0, 6)
             share_weights()
 
-        @pl.when(n == 5)
+        @pl.when(i > 0)
+        def _():
+            service(1, i + 1)
+
+        @pl.when(i == 2)
         def _():
             for copy in own[2]:
                 copy.wait()
@@ -552,37 +570,64 @@
                 copy.wait_recv()
             send_own(2, other, 1)
 
-        @pl.when(n < 2)
-        def _():
-            each_unit(0, n + 6, n + 7, score_unit)
-
-        @pl.when(n >= 2)
-        def _():
-            each_unit(1, n - 2, n - 1, functools.partial(value_unit, 1))
+        @pl.when(i == 1)
+        def _():
+            each_unit(0, 7, 8, score_unit)
+
+        @pl.when(i == 2)
+        def _():
+            send_cache(0, cache_k)
+            each_unit(1, 0, 1, first_values)
 
         return carry
 
-    lax.fori_loop(0, 7, first_step, 0)
-
-    def second_step(n, carry):
-        service(2, n)
-
-        @pl.when(n < 2)
-        def _():
-            each_unit(1, 5 + 2 * n, 7 + n, functools.partial(value_unit, 1))
-
-        @pl.when(n == 1)
+    lax.fori_loop(0, 3, round_c, 0)
+
+    def round_d(i, carry):
+        @pl.when(i < 4)
+        def _():
+            @pl.when(i < 2)
+            def _():
+                service(1, i + 4)
+
+            @pl.when(i >= 2)
+            def _():
+                service(2, i - 2)
+
+        @pl.when(i == 4)
+        def _():
+            service(1, 6)
+
+        @pl.when(i > 4)
+        def _():
+            service(2, i - 3)
+
+        each_unit(1, i + 1, i + 2, first_values)
+
+        @pl.when(i == 6)
         def _():
             finish(0)
             send_cache(1, cache_v.at[0])
 
-        lo = jnp.where(n < 3, 0, 2 * n - 5)
-        hi = jnp.where(n == 6, 7, jnp.where(n < 2, 0, 2 * n - 3))
-        each_unit(2, lo, hi, functools.partial(value_unit, 2))
         return carry
 
-    lax.fori_loop(0, 7, second_step, 0)
-    each_unit(2, 7, 8, functools.partial(value_unit, 2))
+    lax.fori_loop(0, 7, round_d, 0)
+
+    def round_e(i, carry):
+        @pl.when(i < 2)
+        def _():
+            service(2, i + 4)
+
+        @pl.when(i == 3)
+        def _():
+            service(2, 6)
+
+        lo = jnp.where(i == 0, 0, jnp.where(i == 3, 7, 3 * i - 1))
+        hi = jnp.where(i == 3, 8, jnp.where(i == 2, 7, 3 * i + 2))
+        each_unit(2, lo, hi, second_values)
+        return carry
+
+    lax.fori_loop(0, 4, round_e, 0)
     finish(1)
     send_cache(2, cache_v.at[1])
 
@@ -642,15 +687,15 @@
 
 def whole_step(*operands):
     vmem = pl.BlockSpec(memory_space=pltpu.VMEM)
-    hbm = pl.BlockSpec(memory_space=pl.ANY)
-    shape = jax.ShapeDtypeStruct((KV, ROWS), BF)
+    hbm = pl.BlockSpec(memory_space=pltpu.HBM)
+    shape = jax.ShapeDtypeStruct((3 * KV, ROWS), BF)
     dma = pltpu.SemaphoreType.DMA
     buffer = pltpu.VMEM
     return pl.pallas_call(
         step_kernel,
-        out_shape=(shape, shape, shape),
+        out_shape=shape,
         in_specs=[hbm] * 11,
-        out_specs=(vmem, vmem, vmem),
+        out_specs=vmem,
         scratch_shapes=[
             pltpu.SMEM((16,), jnp.int32),
             pltpu.SMEM((16,), jnp.int32),
@@ -696,9 +741,9 @@
             dma((32,)),
         ],
         compiler_params=pltpu.CompilerParams(
-            collective_id=0, has_side_effects=True, vmem_limit_bytes=60 * 1024 * 1024
+            collective_id=0, has_side_effects=True, vmem_limit_bytes=52 * 1024 * 1024
         ),
-    )(*operands)
+    )(*[pltpu.with_memory_space_constraint(x, pltpu.HBM) for x in operands])
 
 
 def shards(
@@ -714,7 +759,7 @@
     placement,
     prefix_owner,
 ):
-    hidden, cache_keys, cache_values = whole_step(
+    out = whole_step(
         suffix_lens,
         req_group,
         prefix_owner,
@@ -727,7 +772,7 @@
         residual.T,
         out_weight,
     )
-    return (hidden.T, cache_keys.T, cache_values.T)
+    return (out[:KV].T, out[KV : 2 * KV].T, out[2 * KV :].T)
 
 
 def solution(mesh):

time: 110 us -> 101 us (0.918)
  Pallas kernels: 105 us -> 99.6 us
  local copies, waits for them, and re-layouts: 4.92 us -> 0.86 us
    pallas_call x1, Pallas kernels: 105 us -> 99.6 us  [whole_step(): pl.pallas_call(step_kernel, out_shape=shape, in_specs=[hbm] * 11, out_spe...]
    unnamed x3 -> x0, local copies, waits for them, and re-layouts: 4.92 us -> none
where the time goes in v3:
time: 101 us
  Pallas kernels  99.6 us (99%)
    pallas_call x1, Pallas kernels, whole_step(): pl.pallas_call(step_kernel, out_shape=shape, in_specs=[hbm] * 11, out_spe...  99.6 us

profile of v3, /device:TPU:1, one launch (start us, length us, event | category | flops | bytes accessed | tf_op | source)
XLA Modules:
  0.0 101.1 jit_solution(15876659656112184360)
XLA Ops:
  0.6 99.6 %shard_map.130 = bf16[1344,256]{1,0:T(8,128)(2,1)S(1)} custom-call(s32[16]{0:T(128)} %lens_hbm.1, s32[16]{0:T(128)} %group_hbm.1, s32[32]{0:T(128)} %owner_hbm.1, s32[64,128]{1,0:T(8,128)} %bitcast.19, bf16[448,256]{1,0:T(8,128)(2,1)} %bitcast.13, bf16[448,256]{1,0:T(8,128)(2,1)} %bitcast.14, bf16[448,256]{1,0:T(8,128)(2,1)} %bitcast.15, ...), custom_call_target="tpu_custom_call" | custom-call | tf_op jit(solution)/shard_map/pallas_call | solution.py:694
  100.3 0.9 slice_bitcast_fusion

commit v4 on v3

--- a/solution.py
+++ b/solution.py
@@ -9,7 +9,8 @@
 from jax.sharding import PartitionSpec as P
 
 HD = 224
-HALF = HD // 2
+CUT = (128, 96)
+CUT_AT = (0, 128)
 ROWS = 256
 PBLK = 128
 PART = ROWS + PBLK
@@ -117,8 +118,9 @@
     mine_lane = pl.multiple_of(xh * PART, 128)
 
     blocks = (keys, vals0, vals1)
-    heights = (HD, HALF, HALF)
-    offsets = (0, 0, HALF)
+    heights = (HD,) + CUT
+    offsets = (0,) + CUT_AT
+    bases = (0, HD, HD + CUT[0])
     suffix = (k_hbm, v_hbm, v_hbm)
     prefix = (pk_hbm, pv_hbm, pv_hbm)
 
@@ -235,6 +237,9 @@
     for copy in own[1]:
         copy.wait()
     send_own(1, xh, 0)
+    for copy in own[2]:
+        copy.wait()
+    send_own(2, xh, 0)
 
     for copy in small[:5]:
         copy.wait()
@@ -274,7 +279,7 @@
     ones = jnp.ones((16, LANES), BF)
     for slot in range(NZ):
         for cc in range(2):
-            vals0[slot, cc, pl.ds(HALF, 16), :] = ones
+            vals0[slot, cc, pl.ds(CUT[0], 16), :] = ones
     exchange_q.wait_recv()
     q_rows[pl.ds(other_q, ROWS), :] = jnp.transpose(q_other[...].astype(F32)).astype(BF)
 
@@ -363,13 +368,14 @@
     def value_unit(f, slot, cc, unit):
         ref = blocks[f]
         which = f - 1
-        factor = jnp.exp2((tops[unit, :, pl.ds(0, 128)] - top[...]) * COEF)
+        factor = jnp.tile(jnp.exp2((tops[unit] - top[...]) * COEF), (1, 2))
         width = ref.shape[2]
         added = dot_nt(weights_ref[unit], ref[slot, cc])
         accum[which, :, pl.ds(0, width)] = (
             accum[which, :, pl.ds(0, width)] + added * factor[:, :width]
         )
-        cache_v[which] = cache_v[which] + moved(ref, HALF, slot, cc, unit)
+        rows = pl.ds(0, CUT[which])
+        cache_v[which, rows, :] = cache_v[which, rows, :] + moved(ref, CUT[which], slot, cc, unit)
 
     def service(f, n):
         k = n // 2 + 1
@@ -397,8 +403,8 @@
         small[5].wait()
         for t in range(TP):
             for half in range(2):
-                w_send[t, :, pl.ds(half * 128, HALF)] = jnp.transpose(
-                    w_ref[pl.ds(half * HALF, HALF), pl.ds(t * KV, KV)].astype(F32)
+                w_send[t, :, pl.ds(CUT_AT[half], CUT[half])] = jnp.transpose(
+                    w_ref[pl.ds(CUT_AT[half], CUT[half]), pl.ds(t * KV, KV)].astype(F32)
                 ).astype(BF)
 
         def send(e, carry):
@@ -442,16 +448,12 @@
     swaps = []
 
     def swap(i, index):
-        height = HD if i == 0 else HALF
-        base = (0, HD, HD + HALF)[i]
-        rows = pl.ds(base, height)
+        rows = pl.ds(bases[i], heights[i])
         return pair_copy(swap_out.at[rows], swap_in.at[rows], 7 + i)
 
     def send_cache(i, ref):
-        height = HD if i == 0 else HALF
-        base = (0, HD, HD + HALF)[i]
+        height, base, offset = heights[i], bases[i], offsets[i]
         out = ck_ref if i == 0 else cv_ref
-        offset = (0, 0, HALF)[i]
 
         @pl.when(xh == 0)
         def _():
@@ -468,8 +470,8 @@
     def att_copy(half, e):
         xx, tt = plane(e)
         return remote(
-            att_out.at[half, xx],
-            att_all.at[half, 2 * tp + xh],
+            att_out.at[half, xx, pl.ds(0, CUT[half])],
+            att_all.at[half, 2 * tp + xh, pl.ds(0, CUT[half])],
             att_send_sem.at[half * 16 + e],
             att_recv_sem.at[half * 16 + e],
             dev(z, xx, core, tt),
@@ -481,25 +483,26 @@
     def att_arrival(half, e):
         head = att_head(e)
         return remote(
-            att_all.at[half, head],
-            att_all.at[half, head],
+            att_all.at[half, head, pl.ds(0, CUT[half])],
+            att_all.at[half, head, pl.ds(0, CUT[half])],
             att_send_sem.at[half * 16 + e],
             att_recv_sem.at[half * 16 + e],
             sibling,
         )
 
     def finish(half):
-        scaled = accum[half, :, pl.ds(0, HALF)] / accum[0, :, pl.ds(HALF, 1)]
+        rows = pl.ds(0, CUT[half])
+        scaled = accum[half, :, rows] / accum[0, :, pl.ds(CUT[0], 1)]
         turned = jnp.transpose(scaled).astype(BF)
-        att_out[half, 0] = turned[:, :ROWS]
-        att_out[half, 1] = turned[:, ROWS:]
+        att_out[half, 0, rows, :] = turned[:, :ROWS]
+        att_out[half, 1, rows, :] = turned[:, ROWS:]
 
         def send(e, carry):
             att_copy(half, e).start()
             return carry
 
         lax.fori_loop(1, 2 * TP, send, 0)
-        att_all[half, 2 * tp + xh] = att_out[half, xh]
+        att_all[half, 2 * tp + xh, rows, :] = att_out[half, xh, rows, :]
 
     def project(half):
         def add(e, carry):
@@ -509,7 +512,8 @@
 
             head = att_head(e)
             projected[...] += dot(
-                w_all[head, :, pl.ds(half * 128, HALF)], att_all[half, head]
+                w_all[head, :, pl.ds(CUT_AT[half], CUT[half])],
+                att_all[half, head, pl.ds(0, CUT[half]), :],
             )
             return carry
 
@@ -555,7 +559,6 @@
         @pl.when(i == 0)
         def _():
             service(0, 6)
-            share_weights()
 
         @pl.when(i > 0)
         def _():
@@ -563,9 +566,6 @@
 
         @pl.when(i == 2)
         def _():
-            for copy in own[2]:
-                copy.wait()
-            send_own(2, xh, 0)
             for copy in exchange[2]:
                 copy.wait_recv()
             send_own(2, other, 1)
@@ -602,13 +602,22 @@
         def _():
             service(2, i - 3)
 
-        each_unit(1, i + 1, i + 2, first_values)
-
-        @pl.when(i == 6)
+        lo = jnp.where(i < 2, 2 * i + 1, jnp.minimum(i + 3, 8))
+        hi = jnp.where(i < 2, 2 * i + 3, jnp.minimum(i + 4, 8))
+        each_unit(1, lo, hi, first_values)
+
+        @pl.when(i == 2)
+        def _():
+            share_weights()
+
+        @pl.when(i == 4)
         def _():
             finish(0)
-            send_cache(1, cache_v.at[0])
-
+            send_cache(1, cache_v.at[0, pl.ds(0, CUT[0])])
+
+        lo = jnp.where(i == 6, 2, 0)
+        hi = jnp.where(i == 6, 3, jnp.where(i == 5, 2, 0))
+        each_unit(2, lo, hi, second_values)
         return carry
 
     lax.fori_loop(0, 7, round_d, 0)
@@ -622,14 +631,14 @@
         def _():
             service(2, 6)
 
-        lo = jnp.where(i == 0, 0, jnp.where(i == 3, 7, 3 * i - 1))
-        hi = jnp.where(i == 3, 8, jnp.where(i == 2, 7, 3 * i + 2))
+        lo = i + 3 + i // 3
+        hi = i + 4 + i // 2
         each_unit(2, lo, hi, second_values)
         return carry
 
     lax.fori_loop(0, 4, round_e, 0)
     finish(1)
-    send_cache(2, cache_v.at[1])
+    send_cache(2, cache_v.at[1, pl.ds(0, CUT[1])])
 
     for e in range(TP):
         w_twin(e, twin).wait_recv()
@@ -639,15 +648,10 @@
     for i in range(3):
         swap(i, 0).wait_recv()
     for i, out in enumerate((ck_ref, cv_ref, cv_ref)):
-        height = HD if i == 0 else HALF
-        base = (0, HD, HD + HALF)[i]
-        offset = (0, 0, HALF)[i]
+        height, base, offset = heights[i], bases[i], offsets[i]
         out[pl.ds(pl.multiple_of(theirs + offset, 16), height), :] = swap_in[
             pl.ds(base, height), :
         ]
-    project(1)
-    hid_ref[...] = projected[...].astype(BF)
-
     for f in range(3):
         for copy in exchange[f]:
             copy.wait_send()
@@ -676,6 +680,9 @@
         return carry
 
     lax.fori_loop(0, TP, drain_weights, 0)
+
+    project(1)
+    hid_ref[...] = projected[...].astype(BF)
 
     def drain_att(e, carry):
         att_copy(0, e).wait_send()
@@ -706,8 +713,8 @@
             buffer((HD, ROWS), BF),
             buffer((HD, ROWS), BF),
             buffer((NZ, 2, HD, LANES), BF),
-            buffer((NZ, 2, HALF + 16, LANES), BF),
-            buffer((NZ, 2, HALF, LANES), BF),
+            buffer((NZ, 2, CUT[0] + 16, LANES), BF),
+            buffer((NZ, 2, CUT[1], LANES), BF),
             buffer((2 * NZ, QN, LANES), BF),
             buffer((2 * NZ, QN, QN), BF),
             buffer((2 * NZ, QN, 128), F32),
@@ -716,15 +723,15 @@
             buffer((QN, 128), jnp.int32),
             buffer((QN, 128), jnp.int32),
             buffer((QN, 128), F32),
-            buffer((2, QN, 128), F32),
+            buffer((2, QN, 256), F32),
             buffer((HD, QN), F32),
-            buffer((2, HALF, QN), F32),
+            buffer((2, CUT[0], QN), F32),
             buffer((KV, ROWS), BF),
             buffer((KV, ROWS), BF),
             buffer((TP, KV, 256), BF),
             buffer((2 * TP, KV, 256), BF),
-            buffer((2, 2, HALF, ROWS), BF),
-            buffer((2, 2 * TP, HALF, ROWS), BF),
+            buffer((2, 2, CUT[0], ROWS), BF),
+            buffer((2, 2 * TP, CUT[0], ROWS), BF),
             buffer((KV, ROWS), F32),
             dma((13,)),
             dma((2, 24)),

time: 101 us -> 97 us (0.960); the launches traced: 101 us -> 95.1 us
  Pallas kernels: 99.6 us -> 93.6 us
    pallas_call x1, Pallas kernels: 99.6 us -> 93.6 us  [whole_step(): pl.pallas_call(step_kernel, out_shape=shape, in_specs=[hbm] * 11, out_spe...]
where the time goes in v4:
time: 97 us; the launch traced here: 95.1 us
  Pallas kernels  93.6 us (96%)
    pallas_call x1, Pallas kernels, whole_step(): pl.pallas_call(step_kernel, out_shape=shape, in_specs=[hbm] * 11, out_spe...  93.6 us

profile of v4, /device:TPU:1, one launch (start us, length us, event | category | flops | bytes accessed | tf_op | source)
XLA Modules:
  0.0 95.1 jit_solution(6975377916790217262)
XLA Ops:
  0.6 93.6 %shard_map.130 = bf16[1344,256]{1,0:T(8,128)(2,1)S(1)} custom-call(s32[16]{0:T(128)} %lens_hbm.1, s32[16]{0:T(128)} %group_hbm.1, s32[32]{0:T(128)} %owner_hbm.1, s32[64,128]{1,0:T(8,128)} %bitcast.19, bf16[448,256]{1,0:T(8,128)(2,1)} %bitcast.13, bf16[448,256]{1,0:T(8,128)(2,1)} %bitcast.14, bf16[448,256]{1,0:T(8,128)(2,1)} %bitcast.15, ...), custom_call_target="tpu_custom_call" | custom-call | tf_op jit(solution)/shard_map/pallas_call | solution.py:701
  94.2 0.9 slice_bitcast_fusion

commit v5 on v4

--- a/solution.py
+++ b/solution.py
@@ -280,6 +280,8 @@
     for slot in range(NZ):
         for cc in range(2):
             vals0[slot, cc, pl.ds(CUT[0], 16), :] = ones
+    for head in range(2 * TP):
+        att_all[1, head, pl.ds(CUT[1], 128 - CUT[1]), :] = jnp.zeros((128 - CUT[1], ROWS), BF)
     exchange_q.wait_recv()
     q_rows[pl.ds(other_q, ROWS), :] = jnp.transpose(q_other[...].astype(F32)).astype(BF)
 
@@ -390,22 +392,26 @@
         def _():
             ring(f, 0, below, part, n + 2).start()
 
+        twin_copy(f, below, part, core).start()
         ring(f, 1, above, part_above, n).wait_recv()
 
         @pl.when((n < 4) | (n == 5))
         def _():
             ring(f, 1, above, part, n + 2 - n // 5).start()
 
-        twin_copy(f, below, part, core).start()
         twin_copy(f, above, part_above, core).start()
 
     def prepare_weights():
         small[5].wait()
         for t in range(TP):
             for half in range(2):
-                w_send[t, :, pl.ds(CUT_AT[half], CUT[half])] = jnp.transpose(
+                turned = jnp.transpose(
                     w_ref[pl.ds(CUT_AT[half], CUT[half]), pl.ds(t * KV, KV)].astype(F32)
                 ).astype(BF)
+                if half == 1:
+                    spare = jnp.zeros((KV, 128 - CUT[1]), BF)
+                    turned = jnp.concatenate([turned, spare], axis=1)
+                w_send[t, :, pl.ds(half * 128, 128)] = turned
 
         def send(e, carry):
             w_copy(e).start()
@@ -505,19 +511,22 @@
         att_all[half, 2 * tp + xh, rows, :] = att_out[half, xh, rows, :]
 
     def project(half):
-        def add(e, carry):
-            @pl.when(e > 0)
-            def _():
-                att_arrival(half, e).wait_recv()
-
-            head = att_head(e)
-            projected[...] += dot(
-                w_all[head, :, pl.ds(CUT_AT[half], CUT[half])],
-                att_all[half, head, pl.ds(0, CUT[half]), :],
-            )
+        def add(g, carry):
+            weights, rows = [], []
+            for j in range(4):
+                e = g * 4 + j
+
+                @pl.when(e > 0)
+                def _(e=e):
+                    att_arrival(half, e).wait_recv()
+
+                head = att_head(e)
+                weights.append(w_all[head, :, pl.ds(half * 128, 128)])
+                rows.append(att_all[half, head])
+            projected[...] += dot(jnp.concatenate(weights, axis=1), jnp.concatenate(rows, axis=0))
             return carry
 
-        lax.fori_loop(0, 2 * TP, add, 0)
+        lax.fori_loop(0, 4, add, 0)
 
     first_values = functools.partial(value_unit, 1)
     second_values = functools.partial(value_unit, 2)

time: 97 us -> 95.3 us (0.982)
  the two profiles are of different devices: /device:TPU:1 before, /device:TPU:33 now
where the time goes in v5:
time: 95.3 us; the launch traced here: 95.2 us
  Pallas kernels  93.7 us (98%)
    pallas_call x1, Pallas kernels, whole_step(): pl.pallas_call(step_kernel, out_shape=shape, in_specs=[hbm] * 11, out_spe...  93.7 us

profile of v5, /device:TPU:33, one launch (start us, length us, event | category | flops | bytes accessed | tf_op | source)
XLA Modules:
  0.0 95.2 jit_solution(1146971529752555097)
XLA Ops:
  0.6 93.7 %shard_map.130 = bf16[1344,256]{1,0:T(8,128)(2,1)S(1)} custom-call(s32[16]{0:T(128)} %lens_hbm.1, s32[16]{0:T(128)} %group_hbm.1, s32[32]{0:T(128)} %owner_hbm.1, s32[64,128]{1,0:T(8,128)} %bitcast.19, bf16[448,256]{1,0:T(8,128)(2,1)} %bitcast.13, bf16[448,256]{1,0:T(8,128)(2,1)} %bitcast.14, bf16[448,256]{1,0:T(8,128)(2,1)} %bitcast.15, ...), custom_call_target="tpu_custom_call" | custom-call | tf_op jit(solution)/shard_map/pallas_call | solution.py:710
  94.3 0.9 slice_bitcast_fusion

commit v6 on v5

--- a/solution.py
+++ b/solution.py
@@ -237,9 +237,6 @@
     for copy in own[1]:
         copy.wait()
     send_own(1, xh, 0)
-    for copy in own[2]:
-        copy.wait()
-    send_own(2, xh, 0)
 
     for copy in small[:5]:
         copy.wait()
@@ -269,9 +266,6 @@
     other_q = pl.multiple_of(other * ROWS, ROWS)
     q_rows[pl.ds(own_q, ROWS), :] = jnp.transpose(q_own[...].astype(F32)).astype(BF)
 
-    for copy in exchange[0]:
-        copy.wait_recv()
-    send_own(0, other, 1)
     top[...] = jnp.full_like(top, NEG)
     accum[...] = jnp.zeros_like(accum)
     cache_k[...] = jnp.zeros_like(cache_k)
@@ -282,6 +276,9 @@
             vals0[slot, cc, pl.ds(CUT[0], 16), :] = ones
     for head in range(2 * TP):
         att_all[1, head, pl.ds(CUT[1], 128 - CUT[1]), :] = jnp.zeros((128 - CUT[1], ROWS), BF)
+    for copy in exchange[0]:
+        copy.wait_recv()
+    send_own(0, other, 1)
     exchange_q.wait_recv()
     q_rows[pl.ds(other_q, ROWS), :] = jnp.transpose(q_other[...].astype(F32)).astype(BF)
 
@@ -543,6 +540,9 @@
             for copy in exchange[1]:
                 copy.wait_recv()
             send_own(1, other, 1)
+            for copy in own[2]:
+                copy.wait()
+            send_own(2, xh, 0)
 
         lo = jnp.where(i == 0, 0, jnp.maximum(i - 1, 1))
         each_unit(0, lo, jnp.maximum(i, 1), score_unit)

time: 95.3 us -> 94.4 us (level)
  the two profiles are of different devices: /device:TPU:33 before, /device:TPU:1 now
where the time goes in v6:
time: 94.4 us; the launch traced here: 94.3 us
  Pallas kernels  92.8 us (98%)
    pallas_call x1, Pallas kernels, whole_step(): pl.pallas_call(step_kernel, out_shape=shape, in_specs=[hbm] * 11, out_spe...  92.8 us

profile of v6, /device:TPU:1, one launch (start us, length us, event | category | flops | bytes accessed | tf_op | source)
XLA Modules:
  0.0 94.3 jit_solution(5977739471723399873)
XLA Ops:
  0.6 92.8 %shard_map.130 = bf16[1344,256]{1,0:T(8,128)(2,1)S(1)} custom-call(s32[16]{0:T(128)} %lens_hbm.1, s32[16]{0:T(128)} %group_hbm.1, s32[32]{0:T(128)} %owner_hbm.1, s32[64,128]{1,0:T(8,128)} %bitcast.19, bf16[448,256]{1,0:T(8,128)(2,1)} %bitcast.13, bf16[448,256]{1,0:T(8,128)(2,1)} %bitcast.14, bf16[448,256]{1,0:T(8,128)(2,1)} %bitcast.15, ...), custom_call_target="tpu_custom_call" | custom-call | tf_op jit(solution)/shard_map/pallas_call | solution.py:710
  93.5 0.9 slice_bitcast_fusion
